TPU v7x, 32 devices: a whole 2x2x4 slice. The times are simulated.
32 devices in a mesh: groups: 2 (over y), context: 4 (over x, core), tensor: 4 (over z).
Axes of the slice: x: 2, y: 2, z: 4, core: 2. Of those that a mesh axis runs over, the one named last changes fastest.
Arguments:
- tokens: bfloat16 [4096, 4096], P(('groups', 'context', 'tensor')), parts along dimension 0, may hold values from -1000 to 1000
- norm_gain: bfloat16 [4096], replicated, may hold values from 0.099609375 to 1.8984375
- w_in: bfloat16 [4096, 3, 4096], P('context', None, 'tensor'), may hold values from -0.09375 to 0.09375
- short_filter: float32 [3, 3, 4096], P(None, None, 'tensor'), may hold values from -3.6 to 3.6
- medium_filter: float32 [128, 4096], P(None, 'tensor'), may hold values from -0.9 to 0.9
- decay: float32 [4096], P('tensor'), may hold values from 0.004 to 0.12
- w_out: bfloat16 [4096, 4096], P('context', 'tensor'), may hold values from -0.09375 to 0.09375
Outputs:
- mixer_out: bfloat16 [4096, 4096], P(('groups', 'context', 'tensor')), parts along dimension 0
There are 2 independent parts, one for each index of `groups`. A program takes and returns all parts, laid end to end along the dimension named above; an argument that names none is the same for every part. Nothing has to cross between parts.
All inputs are finite; a program needn't handle non-finite values.
Results may differ from a plain program's by a relative error of at most 0.01.
Values may be sent and summed in bfloat16 or wider, within the bound.
No kernel may reach another device: no remote copies, remote signals or barrier semaphores. Data moves between devices by JAX's collectives and lax.ppermute only.
A program may use at most 128 MiB of HBM per device.

v0:
```python
import jax
import jax.numpy as jnp
from jax import lax
from jax.sharding import PartitionSpec as P

norm_epsilon = 1e-06
lag_group = 8


def shifted_2(value, axis, steps):
    count = lax.axis_size(axis)
    first, last = (max(0, -steps), min(count, count - steps))
    return lax.ppermute(value, axis, [(source, source + steps) for source in range(first, last)])


def causal_short(extended, short_taps, out_count):
    tap_count = short_taps.shape[0]
    result = short_taps[0][None] * extended[tap_count - 1 : tap_count - 1 + out_count]
    for lag in range(1, tap_count):
        result = (
            result
            + short_taps[lag][None]
            * extended[tap_count - 1 - lag : tap_count - 1 - lag + out_count]
        )
    return result


def local(tokens, norm_gain, w_in, short_filter, medium_filter, decay, w_out):
    values = tokens.astype(jnp.float32)
    inverse_rms = lax.rsqrt(jnp.mean(values * values, axis=1, keepdims=True) + norm_epsilon)
    normed = (values * inverse_rms * norm_gain.astype(jnp.float32)[None, :]).astype(jnp.bfloat16)
    gathered = lax.all_gather(normed, "tensor", axis=0, tiled=True)
    slab_length = gathered.shape[0]
    channels = w_in.shape[2]
    shard_rows = lax.all_gather(w_in, "context", axis=0, tiled=True)
    row_count = shard_rows.shape[0]
    projection_acc = jnp.dot(
        gathered, shard_rows.reshape(row_count, 3 * channels), preferred_element_type=jnp.float32
    )
    projected = projection_acc.astype(jnp.bfloat16).reshape(slab_length, 3, channels)
    short_taps = short_filter.shape[0]
    medium_taps = medium_filter.shape[0]
    short_edge = shifted_2(projected[slab_length - (short_taps - 1) :], "context", 1)
    featured = causal_short(
        jnp.concatenate([short_edge, projected], axis=0).astype(jnp.float32),
        short_filter,
        slab_length,
    )
    query_feat = featured[:, 0]
    gated = (featured[:, 1] * featured[:, 2]).astype(jnp.bfloat16)
    gated_edge = shifted_2(gated[slab_length - (medium_taps - 1) :], "context", 1)
    gated_ext = jnp.concatenate([gated_edge, gated], axis=0)
    lag_index = jnp.arange(medium_taps, dtype=jnp.float32)
    filter_taps = (medium_filter * jnp.exp(-decay[None, :] * lag_index[:, None])).astype(
        jnp.bfloat16
    )

    def add_lags(turn, total):
        first_lag = turn * lag_group
        for offset in range(lag_group):
            lag = first_lag + offset
            shifted = lax.dynamic_slice_in_dim(gated_ext, medium_taps - 1 - lag, slab_length, 0)
            weights = lax.dynamic_slice_in_dim(filter_taps, lag, 1, 0)
            total = total + weights.astype(jnp.float32) * shifted.astype(jnp.float32)
        return total

    mixed = lax.fori_loop(
        0, medium_taps // lag_group, add_lags, jnp.zeros((slab_length, channels), jnp.float32)
    )
    combined = (query_feat * mixed).astype(jnp.bfloat16)
    out_full = lax.all_gather(w_out, "context", axis=0, tiled=True)
    return lax.psum_scatter(
        lax.dot_general(
            combined, out_full, (((1,), (1,)), ((), ())), preferred_element_type=jnp.float32
        ).astype(jnp.bfloat16),
        "tensor",
        scatter_dimension=0,
        tiled=True,
    )


def solution(mesh):
    in_specs = (
        P(("groups", "context", "tensor"), None),
        P(),
        P("context", None, "tensor"),
        P(None, None, "tensor"),
        P(None, "tensor"),
        P("tensor"),
        P("context", "tensor"),
    )
    out_specs = P(("groups", "context", "tensor"), None)
    return jax.shard_map(local, mesh=mesh, in_specs=in_specs, out_specs=out_specs, check_vma=False)
```

profile of v0, /device:TPU:0, one launch (start us, length us, event | category | flops | bytes accessed | tf_op | source)
XLA Modules:
  0.0 461.0 jit_solution(12642814142959749235)
XLA Ops:
  8.8 2.5 fusion.11
  11.4 8.6 %copy.10 = bf16[1024,3,1024]{0,2,1:T(8,128)(2,1)} copy(bf16[1024,3,1024]{2,0,1:T(8,128)(2,1)} %param.11) | data formatting | bytes 12582912 | tf_op args[2]
  21.9 73.0 %all-gather.4.cloned.1.call-done = bf16[512,4096]{1,0:T(8,128)(2,1)} async-done(((bf16[128,4096]{1,0:T(8,128)(2,1)}), bf16[512,4096]{1,0:T(8,128)(2,1)}) %all-gather.4.cloned.1.call-update) | async-done | bytes 4194320 | tf_op jit(solution)/shard_map/all_gather | solution.py:32
  94.9 154.9 %all-gather.6.cloned.1.call-done = bf16[4096,3,1024]{0,2,1:T(8,128)(2,1)} async-done(((bf16[1024,3,1024]{0,2,1:T(8,128)(2,1)}), bf16[4096,3,1024]{0,2,1:T(8,128)(2,1)}) %all-gather.6.cloned.1.call-update) | async-done | bytes 25165840 | tf_op jit(solution)/shard_map/all_gather | solution.py:35
  249.9 18.4 %convolution_convert_fusion.1 = bf16[512,3072]{1,0:T(8,128)(2,1)S(1)} fusion(bf16[512,4096]{1,0:T(8,128)(2,1)} %all-gather.4.cloned.1.call-done, bf16[4096,3072]{0,1:T(8,128)(2,1)} %bitcast.55), kind=kOutput, calls=%fused_computation.22 | convolution fusion | flops 12886474752 | bytes 32505856 | tf_op jit(solution)/shard_map/dot_general | solution.py:37
  268.4 2.1 collective-permute-start
  270.6 4.7 %copy.11 = bf16[512,3072]{0,1:T(8,128)(2,1)} copy(bf16[512,3072]{1,0:T(8,128)(2,1)} %copy-done.1) | data formatting | bytes 6291456 | tf_op jit(solution)/shard_map/convert_element_type | solution.py:40
  275.7 3.6 maximum_convert_fusion
  279.3 5.6 %fusion.7 = f32[512,3,1024]{0,2,1:T(8,128)S(1)} fusion(f32[514,3,1024]{0,2,1:T(8,128)S(1)} %maximum_convert_fusion, f32[3,1024]{1,0:T(4,128)S(1)} %get-tuple-element.193, f32[3,1024]{1,0:T(4,128)S(1)} %get-tuple-element.194, f32[3,1024]{1,0:T(4,128)S(1)} %get-tuple-element.192), kind=kLoop, calls=%fused_computation.17 | loop fusion | flops 7864320 | bytes 25202688 | tf_op jit(solution)/shard_map/add | solution.py:21
  285.4 2.1 collective-permute-start.1
  288.5 1.7 pad_maximum_fusion
  290.2 1.6 copy.13
  291.8 62.5 %while.17 = (s32[]{:T(128)}, f32[512,1024]{1,0:T(8,128)S(1)}, bf16[128,1024]{1,0:T(8,128)(2,1)}, bf16[639,1024]{1,0:T(8,128)(2,1)S(1)}, s32[]{:T(128)}, /*index=...) while((s32[]{:T(128)}, f32[512,1024]{1,0:T(8,128)S(1)}, ...), condition=%wide.region_2.0_spmd.clone, body=%wide.region_1.0_spmd.clone.sunk | while | flops 13115459 | bytes 12665847 | solution.py:67
  293.0 2.7 fusion.21
  296.9 2.7 fusion.21
  300.8 2.7 fusion.21
  304.7 2.7 fusion.21
  308.6 2.7 fusion.21
  312.5 2.7 fusion.21
  316.4 2.7 fusion.21
  320.3 2.7 fusion.21
  324.2 2.7 fusion.21
  328.1 2.7 fusion.21
  332.2 2.7 fusion.21
  336.1 2.7 fusion.21
  340.0 2.7 fusion.21
  343.9 2.7 fusion.21
  347.7 2.7 fusion.21
  351.6 2.7 fusion.21
  354.3 1.9 copy.14
  356.2 11.3 %convolution_convert_fusion = bf16[512,4096]{1,0:T(8,128)(2,1)} fusion(bf16[4096,1024]{1,0:T(8,128)(2,1)} %all-gather.8.cloned.1.call-done, f32[512,1024]{0,1:T(8,128)} %copy.14, f32[512,3,1024]{0,2,1:T(8,128)} %copy-done), kind=kOutput, calls=%fused_computation.21 | convolution fusion | flops 4298113024 | bytes 16777216 | tf_op jit(solution)/shard_map/dot_general | solution.py:73
  367.5 86.9 %reduce-scatter.2.cloned.1.call-done = bf16[128,4096]{1,0:T(8,128)(2,1)} async-done(((bf16[512,4096]{1,0:T(8,128)(2,1)}), bf16[128,4096]{1,0:T(8,128)(2,1)}) %reduce-scatter.2.cloned.1.call-update) | async-done | bytes 1048592 | tf_op jit(solution)/shard_map/reduce_scatter | solution.py:72
  (50 shorter events, 23.2 us)
Async XLA Ops:
  6.5 88.4 %all-gather.4.cloned.1.call-start = ((), (), s32[]{:S(2)}) async-start(), calls=%async_computation.1 | async-start | bytes 5242880 | tf_op jit(solution)/shard_map/all_gather | solution.py:32
  11.3 238.6 %all-gather.6.cloned.1.call-start = ((), (), s32[]{:S(2)}) async-start(), calls=%async_computation.2 | async-start | bytes 31457280 | tf_op jit(solution)/shard_map/all_gather | solution.py:35
  20.0 0.8 copy-start.4
  20.0 1.1 copy-start.2
  20.0 336.2 %all-gather.8.cloned.1.call-start = ((), (), s32[]{:S(2)}) async-start(), calls=%async_computation.3 | async-start | bytes 10485760 | tf_op jit(solution)/shard_map/all_gather | solution.py:71
  20.8 433.6 %reduce-scatter.2.cloned.1.call-start = ((), (), s32[]{:S(2)}) async-start(), calls=%async_computation.4 | async-start | bytes 5242880 | tf_op jit(solution)/shard_map/reduce_scatter | solution.py:72
  249.9 20.7 %copy-start.3 = (f32[3,3,1024]{2,1,0:T(4,128)S(1)}, f32[3,3,1024]{2,1,0:T(4,128)}, u32[]{:S(2)}) copy-start(f32[3,3,1024]{2,1,0:T(4,128)} %param.12) | copy-start | bytes 110596
  268.3 2.2 copy-start.1
  268.4 6.9 %collective-permute-start = (bf16[2,3,1024]{2,1,0:T(4,128)(2,1)S(1)}, bf16[2,3,1024]{2,1,0:T(4,128)(2,1)S(1)}, u32[]{:S(2)}, u32[]{:S(2)}) collective-permute-start(bf16[2,3,1024]{2,1,0:T(4,128)(2,1)S(1)} %slice.41), channel_id=1, source_target_pairs={{0,4},{4,8},{8,12},{1,5},{5,9},{9,13},{2,6},{6,10},{10,14},{3,7},{... | collective-permute-start | bytes 36872 | tf_op jit(solution)/shard_map/ppermute | solution.py:13
  284.9 3.6 copy-start
  285.4 3.1 collective-permute-start.1
Sparse Core Ops, SparseCore 0:
  11.4 83.4 all-gather.3
  96.5 153.3 all-gather.5
  251.4 58.2 all-gather.7
  367.6 86.7 reduce-scatter.1
where the time goes:
time: 463 us; the launch traced here: 461 us
  waiting for transfers between devices  316 us (68%)
  other arithmetic  77.4 us (17%)
  matrix products  29.7 us (6%)
  local copies, waits for them, and re-layouts  17.7 us (4%)
  between operations  13.3 us (3%)
    all_gather x1, waiting for transfers between devices, local(): shard_rows = lax.all_gather(w_in, 'context', axis=0, tiled=True)  155 us
    reduce_scatter x1, waiting for transfers between devices, local(): lax.psum_scatter(lax.dot_general(combined, out_full, (((1,), (1,)), ((),...  86.9 us
    all_gather x1, waiting for transfers between devices, local(): gathered = lax.all_gather(normed, 'tensor', axis=0, tiled=True)  73 us
    add x16, other arithmetic, add_lags(): total = total + weights.astype(jnp.float32) * shifted.astype(jnp.float32)  43.1 us
    dot_general x1, matrix products, local(): jnp.dot(gathered, shard_rows.reshape(row_count, 3 * channels), preferred_...  18.4 us
    mul x16, other arithmetic, add_lags(): total = total + weights.astype(jnp.float32) * shifted.astype(jnp.float32)  17.1 us
    dot_general x1, matrix products, local(): lax.dot_general(combined, out_full, (((1,), (1,)), ((), ())), preferred_e...  11.3 us
    unnamed x12, local copies, waits for them, and re-layouts  10.5 us
  transfers between devices with their start and end apart: 6, of which 4 were waited for; matrix products, arithmetic and copies ran while one was open for 24% of the time, Pallas kernels for 0%

commit v1 on v0

--- a/solution.py
+++ b/solution.py
@@ -29,7 +29,14 @@
     values = tokens.astype(jnp.float32)
     inverse_rms = lax.rsqrt(jnp.mean(values * values, axis=1, keepdims=True) + norm_epsilon)
     normed = (values * inverse_rms * norm_gain.astype(jnp.float32)[None, :]).astype(jnp.bfloat16)
-    gathered = lax.all_gather(normed, "tensor", axis=0, tiled=True)
+    ring = [normed]
+    for hop in range(3):
+        ring.append(lax.ppermute(ring[-1], "tensor", [(dev, (dev + 1) % 4) for dev in range(4)]))
+    gathered = jnp.roll(
+        jnp.concatenate(ring[::-1], axis=0),
+        (lax.axis_index("tensor") + 1) * ring[0].shape[0],
+        axis=0,
+    )
     slab_length = gathered.shape[0]
     channels = w_in.shape[2]
     shard_rows = lax.all_gather(w_in, "context", axis=0, tiled=True)

time: 463 us -> 387 us (0.84)
  waiting for transfers between devices: 316 us -> 227 us
  local copies, waits for them, and re-layouts: 17.7 us -> 29 us
    all_gather x1, waiting for transfers between devices: 155 us -> 64.6 us  [local(): shard_rows = lax.all_gather(w_in, 'context', axis=0, tiled=True)]
    ppermute x0 -> x3, waiting for transfers between devices: none -> 74.7 us  [local(): lax.ppermute(ring[-1], 'tensor', [(dev, (dev + 1) % 4) for dev in range(4)])]
    all_gather x1 -> x0, waiting for transfers between devices: 73 us -> none  [local(): gathered = lax.all_gather(normed, 'tensor', axis=0, tiled=True)]
    unnamed x12 -> x20, local copies, waits for them, and re-layouts: 10.5 us -> 21.9 us
  transfers between devices with their start and end apart: 6 -> 8, of which waited for: 4 -> 6; matrix products, arithmetic and copies ran while one was open for 24% -> 29% of each run, Pallas kernels for 0% -> 0%
where the time goes in v1:
time: 387 us; the launch traced here: 385 us
  waiting for transfers between devices  227 us (59%)
  other arithmetic  76.8 us (20%)
  matrix products  29.7 us (8%)
  local copies, waits for them, and re-layouts  29 us (7%)
  between operations  13.3 us (3%)
  starting transfers between devices  7.49 us (2%)
    reduce_scatter x1, waiting for transfers between devices, local(): lax.psum_scatter(lax.dot_general(combined, out_full, (((1,), (1,)), ((),...  86.8 us
    ppermute x3, waiting for transfers between devices, local(): lax.ppermute(ring[-1], 'tensor', [(dev, (dev + 1) % 4) for dev in range(4)])  74.7 us
    all_gather x1, waiting for transfers between devices, local(): shard_rows = lax.all_gather(w_in, 'context', axis=0, tiled=True)  64.6 us
    add x16, other arithmetic, add_lags(): total = total + weights.astype(jnp.float32) * shifted.astype(jnp.float32)  43.1 us
    unnamed x20, local copies, waits for them, and re-layouts  21.9 us
    dot_general x1, matrix products, local(): jnp.dot(gathered, shard_rows.reshape(row_count, 3 * channels), preferred_...  18.4 us
    mul x16, other arithmetic, add_lags(): total = total + weights.astype(jnp.float32) * shifted.astype(jnp.float32)  16.9 us
    dot_general x1, matrix products, local(): lax.dot_general(combined, out_full, (((1,), (1,)), ((), ())), preferred_e...  11.3 us
  transfers between devices with their start and end apart: 8, of which 6 were waited for; matrix products, arithmetic and copies ran while one was open for 29% of the time, Pallas kernels for 0%

profile of v1, /device:TPU:0, one launch (start us, length us, event | category | flops | bytes accessed | tf_op | source)
XLA Modules:
  0.0 385.4 jit_solution(17510023904656719225)
XLA Ops:
  6.5 8.6 %copy.10 = bf16[1024,3,1024]{0,2,1:T(8,128)(2,1)} copy(bf16[1024,3,1024]{2,0,1:T(8,128)(2,1)} %param.11) | data formatting | bytes 12582912 | tf_op args[2]
  17.1 3.1 collective-permute-start
  20.1 25.2 %collective-permute-done = bf16[128,4096]{1,0:T(8,128)(2,1)S(1)} collective-permute-done((bf16[128,4096]{1,0:T(8,128)(2,1)S(1)}, bf16[128,4096]{1,0:T(8,128)(2,1)S(1)}, u32[]{:S(2)}, u32[]{:S(2)}) %collective-permute-start) | collective-permute-done | bytes 1048608 | tf_op jit(solution)/shard_map/ppermute | solution.py:34
  45.3 26.1 %collective-permute-done.1 = bf16[128,4096]{1,0:T(8,128)(2,1)S(1)} collective-permute-done((bf16[128,4096]{1,0:T(8,128)(2,1)S(1)}, bf16[128,4096]{1,0:T(8,128)(2,1)S(1)}, u32[]{:S(2)}, u32[]{:S(2)}) %collective-permute-start.1) | collective-permute-done | bytes 1048608 | tf_op jit(solution)/shard_map/ppermute | solution.py:34
  73.4 23.4 %collective-permute-done.2 = bf16[128,4096]{1,0:T(8,128)(2,1)} collective-permute-done((bf16[128,4096]{1,0:T(8,128)(2,1)S(1)}, bf16[128,4096]{1,0:T(8,128)(2,1)}, u32[]{:S(2)}, u32[]{:S(2)}) %collective-permute-start.2) | collective-permute-done | bytes 1048608 | tf_op jit(solution)/shard_map/ppermute | solution.py:34
  96.8 2.3 constant_dynamic-update-slice_fusion.7
  102.5 2.3 constant_dynamic-update-slice_fusion.3
  108.3 64.6 %all-gather.3.cloned.1.call-done = bf16[4096,3,1024]{0,2,1:T(8,128)(2,1)} async-done(((bf16[1024,3,1024]{0,2,1:T(8,128)(2,1)}), bf16[4096,3,1024]{0,2,1:T(8,128)(2,1)}) %all-gather.3.cloned.1.call-update) | async-done | bytes 25165840 | tf_op jit(solution)/shard_map/all_gather | solution.py:42
  172.9 18.4 %convolution_convert_fusion.1 = bf16[512,3072]{1,0:T(8,128)(2,1)S(1)} fusion(bf16[4096,3072]{0,1:T(8,128)(2,1)} %bitcast.54, bf16[1024,4096]{1,0:T(8,128)(2,1)} %constant_dynamic-update-slice_fusion, s32[]{:T(128)S(6)} %select_n.190), kind=kOutput, calls=%fused_computation.22 | convolution fusion | flops 12886474752 | bytes 32505860 | tf_op jit(solution)/shard_map/dot_general | solution.py:44
  195.2 4.7 %copy.11 = bf16[512,3072]{0,1:T(8,128)(2,1)} copy(bf16[512,3072]{1,0:T(8,128)(2,1)} %copy-done.2) | data formatting | bytes 6291456 | tf_op jit(solution)/shard_map/convert_element_type | solution.py:47
  200.3 3.6 maximum_convert_fusion
  203.9 5.6 %fusion.7 = f32[512,3,1024]{0,2,1:T(8,128)S(1)} fusion(f32[514,3,1024]{0,2,1:T(8,128)S(1)} %maximum_convert_fusion, f32[3,1024]{1,0:T(4,128)S(1)} %get-tuple-element.193, f32[3,1024]{1,0:T(4,128)S(1)} %get-tuple-element.194, f32[3,1024]{1,0:T(4,128)S(1)} %get-tuple-element.192), kind=kLoop, calls=%fused_computation.17 | loop fusion | flops 7864320 | bytes 25202688 | tf_op jit(solution)/shard_map/add | solution.py:21
  210.0 2.2 collective-permute-start.4
  216.6 62.3 %while.17 = (s32[]{:T(128)}, f32[512,1024]{1,0:T(8,128)S(1)}, bf16[128,1024]{1,0:T(8,128)(2,1)}, bf16[639,1024]{1,0:T(8,128)(2,1)S(1)}, s32[]{:T(128)}, /*index=...) while((s32[]{:T(128)}, f32[512,1024]{1,0:T(8,128)S(1)}, ...), condition=%wide.region_2.3_spmd.clone, body=%wide.region_1.2_spmd.clone.sunk | while | flops 13115459 | bytes 12665847 | solution.py:74
  217.8 2.7 fusion.22
  221.7 2.7 fusion.22
  225.6 2.7 fusion.22
  229.4 2.7 fusion.22
  233.3 2.7 fusion.22
  237.2 2.7 fusion.22
  241.1 2.7 fusion.22
  245.0 2.7 fusion.22
  248.9 2.7 fusion.22
  252.8 2.7 fusion.22
  256.7 2.7 fusion.22
  260.6 2.7 fusion.22
  264.5 2.7 fusion.22
  268.4 2.7 fusion.22
  272.3 2.7 fusion.22
  276.2 2.7 fusion.22
  280.7 11.3 %convolution_convert_fusion = bf16[512,4096]{1,0:T(8,128)(2,1)} fusion(bf16[4096,1024]{1,0:T(8,128)(2,1)} %all-gather.5.cloned.1.call-done, f32[512,1024]{0,1:T(8,128)} %copy.14, f32[512,3,1024]{0,2,1:T(8,128)} %copy-done), kind=kOutput, calls=%fused_computation.21 | convolution fusion | flops 4298113024 | bytes 16777216 | tf_op jit(solution)/shard_map/dot_general | solution.py:80
  292.0 86.8 %reduce-scatter.2.cloned.1.call-done = bf16[128,4096]{1,0:T(8,128)(2,1)} async-done(((bf16[512,4096]{1,0:T(8,128)(2,1)}), bf16[128,4096]{1,0:T(8,128)(2,1)}) %reduce-scatter.2.cloned.1.call-update) | async-done | bytes 1048592 | tf_op jit(solution)/shard_map/reduce_scatter | solution.py:79
  (63 shorter events, 38.5 us)
Async XLA Ops:
  6.5 166.3 %all-gather.3.cloned.1.call-start = ((), (), s32[]{:S(2)}) async-start(), calls=%async_computation.1 | async-start | bytes 31457280 | tf_op jit(solution)/shard_map/all_gather | solution.py:42
  15.2 0.7 copy-start.4
  15.2 1.2 copy-start.1
  15.2 265.5 %all-gather.5.cloned.1.call-start = ((), (), s32[]{:S(2)}) async-start(), calls=%async_computation.2 | async-start | bytes 10485760 | tf_op jit(solution)/shard_map/all_gather | solution.py:78
  16.7 54.8 %copy-start.5 = (f32[1024]{0:T(1024)S(1)}, f32[1024]{0:T(1024)}, u32[]{:S(2)}) copy-start(f32[1024]{0:T(1024)} %param.14) | copy-start | bytes 12292
  17.1 28.3 %collective-permute-start = (bf16[128,4096]{1,0:T(8,128)(2,1)S(1)}, bf16[128,4096]{1,0:T(8,128)(2,1)S(1)}, u32[]{:S(2)}, u32[]{:S(2)}) collective-permute-start(bf16[128,4096]{1,0:T(8,128)(2,1)S(1)} %fusion.12), channel_id=1, source_target_pairs={{0,1},{1,2},{2,3},{3,0},{4,5},{5,6},{6,7},{7,4},{8,9},{9,10},{10,1... | collective-permute-start | bytes 3145736 | tf_op jit(solution)/shard_map/ppermute | solution.py:34
  45.3 26.1 %collective-permute-start.1 = (bf16[128,4096]{1,0:T(8,128)(2,1)S(1)}, bf16[128,4096]{1,0:T(8,128)(2,1)S(1)}, u32[]{:S(2)}, u32[]{:S(2)}) collective-permute-start(bf16[128,4096]{1,0:T(8,128)(2,1)S(1)} %collective-permute-done), channel_id=1, source_target_pairs={{0,1},{1,2},{2,3},{3,0},{4,5},{5,6},{6,7},{7,4},{8,9},{9,10},{10,1... | collective-permute-start | bytes 3145736 | tf_op jit(solution)/shard_map/ppermute | solution.py:34
  71.5 25.3 %collective-permute-start.2 = (bf16[128,4096]{1,0:T(8,128)(2,1)S(1)}, bf16[128,4096]{1,0:T(8,128)(2,1)}, u32[]{:S(2)}, u32[]{:S(2)}) collective-permute-start(bf16[128,4096]{1,0:T(8,128)(2,1)S(1)} %collective-permute-done.1), channel_id=1, source_target_pairs={{0,1},{1,2},{2,3},{3,0},{4,5},{5,6},{6,7},{7,4},{8,9},{9,10},{10,1... | collective-permute-start | bytes 3145736 | tf_op jit(solution)/shard_map/ppermute | solution.py:34
  71.5 307.4 %reduce-scatter.2.cloned.1.call-start = ((), (), s32[]{:S(2)}) async-start(), calls=%async_computation.3 | async-start | bytes 5242880 | tf_op jit(solution)/shard_map/reduce_scatter | solution.py:79
  172.9 22.3 %copy-start.3 = (f32[3,3,1024]{2,1,0:T(4,128)S(1)}, f32[3,3,1024]{2,1,0:T(4,128)}, u32[]{:S(2)}) copy-start(f32[3,3,1024]{2,1,0:T(4,128)} %param.12) | copy-start | bytes 110596
  191.3 1.7 copy-start.2
  193.0 6.9 %collective-permute-start.3 = (bf16[2,3,1024]{2,1,0:T(4,128)(2,1)S(1)}, bf16[2,3,1024]{2,1,0:T(4,128)(2,1)S(1)}, u32[]{:S(2)}, u32[]{:S(2)}) collective-permute-start(bf16[2,3,1024]{2,1,0:T(4,128)(2,1)S(1)} %slice.41), channel_id=1, source_target_pairs={{0,4},{4,8},{8,12},{1,5},{5,9},{9,13},{2,6},{6,10},{10,14},{3,7},{... | collective-permute-start | bytes 36872 | tf_op jit(solution)/shard_map/ppermute | solution.py:13
  209.5 3.7 copy-start
  210.0 3.1 collective-permute-start.4
Sparse Core Ops, SparseCore 0:
  15.3 157.4 all-gather.2
  174.4 58.2 all-gather.4
  292.2 86.6 reduce-scatter.1
